TPU v7x, 256 devices: a whole 4x4x8 slice. The times are simulated.
256 devices in a mesh: shard: 8 (over z_lo, x), tensor: 4 (over z_hi), section: 8 (over y, core).
Axes of the slice: x: 4, y: 4, z: 8 (z_hi: 4, z_lo: 2; z = z_hi * 2 + z_lo), core: 2. Of those that a mesh axis runs over, the one named last changes fastest.
Arguments:
- activations: bfloat16 [8, 2048, 2304], P(None, 'shard', ('tensor', 'section')), may hold values from -6 to 6
- router_grad: bfloat16 [8, 2048], P(None, 'shard'), may hold values from -6 to 6
- token_ids: int32 [2048], P('shard'), may hold values from 0 to 8191
- norm_terms: bfloat16 [2, 2048, 2304], P(None, 'shard', ('tensor', 'section'))
- old_factors: float32 [8, 2304, 2304], P('shard', 'tensor', 'section'), as said below
- old_router_factor: float32 [8, 8], replicated, as said below
- old_norm_diag: float32 [2, 2304], P(None, ('tensor', 'section')), may hold values from 0.5 to 5
- old_embed_diag: float32 [8192], P('tensor'), may hold values from 0.05 to 0.5
Outputs:
- precond_attn: float32 [4, 2304, 2304], P(None, 'tensor', 'section')
- precond_router: float32 [8, 2304], P(None, 'tensor')
- precond_norms: float32 [2, 2304], P(None, ('tensor', 'section'))
- precond_embed: float32 [8192, 2304], P('tensor', 'section')
Inputs may be any that keep to these rules, and one draw needn't show every extreme that they name: `old_factors`: each matrix is symmetric with a positive diagonal. `old_router_factor`: symmetric with a positive diagonal.
All inputs are finite; a program needn't handle non-finite values.
Results may differ from a plain program's by a relative error of at most 0.0083.
Values may be sent and summed in bfloat16 or wider, within the bound.
A program may use at most 64 MiB of HBM per device.

v0:
```python
import math
import jax
import jax.numpy as jnp
from jax import lax
from jax.sharding import PartitionSpec as P

D = 2304
EXPERTS = 8
VOCAB = 8192
factor_decay = 0.5
damping = 0.01
learning_rate = 0.05


def local_inverse(matrix):
    width = matrix.shape[0]
    trace = jnp.sum(jnp.diagonal(matrix))
    factor_scale = width / (3.0 * trace)
    identity = jnp.eye(width, dtype=jnp.float32)
    matrix_low = lax.optimization_barrier(matrix.astype(jnp.bfloat16))
    first = 2.0 * factor_scale * identity - factor_scale * factor_scale * matrix_low.astype(
        jnp.float32
    )
    first_low = first.astype(jnp.bfloat16)
    image = jnp.dot(matrix_low, first_low, preferred_element_type=jnp.float32).astype(jnp.bfloat16)
    product = jnp.dot(first_low, image, preferred_element_type=jnp.float32)
    return (2.0 * first - product).astype(jnp.bfloat16)


def fold_with(columns, piece):
    return jnp.einsum("kij,kjl->kil", piece, columns, preferred_element_type=jnp.float32)


def per_device(
    activations,
    router_grad,
    token_ids,
    norm_terms,
    old_factors,
    old_router_factor,
    old_norm_diag,
    old_embed_diag,
):
    n_tensor = lax.axis_size("tensor")
    n_section = lax.axis_size("section")
    n_shard = lax.axis_size("shard")
    tensor_rank = lax.axis_index("tensor")
    section_rank = lax.axis_index("section")
    row_block = D // n_tensor
    col_block = D // n_section
    tokens_all = activations.shape[1] * n_shard
    row_start = tensor_rank * row_block
    col_start = section_rank * col_block

    def collect(carry, piece):
        whole = lax.all_gather(piece, ("tensor", "section"), axis=1, tiled=True)
        rows_part = lax.dynamic_slice_in_dim(whole, row_start, row_block, 1)
        cols_part = lax.dynamic_slice_in_dim(whole, col_start, col_block, 1)
        return (carry, (rows_part, cols_part))

    unused_carry, (row_parts, col_parts) = lax.scan(collect, jnp.int32(0), activations)
    partial_value = jnp.einsum(
        "mnr,mnc->mrc", row_parts, col_parts, preferred_element_type=jnp.float32
    )
    fresh = lax.psum_scatter(partial_value, "shard", scatter_dimension=0, tiled=True) / tokens_all
    row_index = lax.broadcasted_iota(jnp.int32, (row_block, col_block), 0) + row_start
    col_index = lax.broadcasted_iota(jnp.int32, (row_block, col_block), 1) + col_start
    eye_block = (row_index == col_index).astype(jnp.float32)
    matrix = factor_decay * old_factors + (1.0 - factor_decay) * fresh + damping * eye_block
    diag_part = jnp.sum(matrix * eye_block, axis=(1, 2))
    trace = lax.psum(diag_part, ("tensor", "section"))
    factor_scale = (D / (3.0 * trace))[:, None, None]
    matrix_low = lax.optimization_barrier(matrix.astype(jnp.bfloat16))
    first = 2.0 * factor_scale * eye_block - factor_scale * factor_scale * matrix_low.astype(
        jnp.float32
    )
    first_low = first.astype(jnp.bfloat16)
    first_cols = lax.all_gather(first_low, "tensor", axis=1, tiled=True)
    image = fold_with(first_cols, lax.all_gather(matrix_low, "section", axis=2, tiled=True))
    image_cols = lax.all_gather(image.astype(jnp.bfloat16), "tensor", axis=1, tiled=True)
    product = fold_with(image_cols, lax.all_gather(first_low, "section", axis=2, tiled=True))
    inverse_low = (2.0 * first - product).astype(jnp.bfloat16)
    inverses = lax.all_gather(inverse_low, "shard", axis=0, tiled=True)
    left_terms = jnp.stack(
        [
            jnp.einsum("nc,rc->nr", col_parts[m], inverses[m], preferred_element_type=jnp.float32)
            for m in (0, 4, 6)
        ]
    )
    left = lax.psum(left_terms, "section").astype(jnp.bfloat16)
    right_terms = jnp.stack(
        [
            jnp.einsum("nr,rc->nc", row_parts[m], inverses[m], preferred_element_type=jnp.float32)
            for m in (1, 2, 3, 5, 7)
        ]
    )
    right = lax.psum(right_terms, "tensor").astype(jnp.bfloat16)
    norm_values = norm_terms.astype(jnp.float32)
    router_part = jnp.einsum(
        "en,fn->ef", router_grad, router_grad, preferred_element_type=jnp.float32
    )
    router_sum, norm_total, norm_squares = lax.psum(
        (router_part, jnp.sum(norm_values, axis=1), jnp.sum(norm_values * norm_values, axis=1)),
        "shard",
    )
    router_matrix = (
        factor_decay * old_router_factor
        + (1.0 - factor_decay) * (router_sum / tokens_all)
        + damping * jnp.eye(EXPERTS, dtype=jnp.float32)
    )
    router_inverse = local_inverse(router_matrix)
    router_right = jnp.einsum(
        "en,ef->nf", router_grad, router_inverse, preferred_element_type=jnp.float32
    ).astype(jnp.bfloat16)
    precond_norms = (
        learning_rate
        * norm_total
        / (
            factor_decay * old_norm_diag
            + (1.0 - factor_decay) * (norm_squares / tokens_all)
            + damping
        )
    )
    ids_all = lax.all_gather(token_ids, "shard", axis=0, tiled=True)
    embed_all = lax.all_gather(right[4], "shard", axis=0, tiled=True)
    paired_left = jnp.stack([left[0], left[0], left[0], left[1]])
    attn_terms = jnp.einsum(
        "wnr,wnc->wrc", paired_left, right[:4], preferred_element_type=jnp.float32
    )
    router_term = jnp.einsum("nf,nr->fr", router_right, left[2], preferred_element_type=jnp.float32)
    attn_sum, router_total = lax.psum((attn_terms, router_term), "shard")
    precond_attn = learning_rate * attn_sum
    precond_router = learning_rate * router_total
    vocab_block = VOCAB // n_tensor
    step_rows = math.gcd(vocab_block, 512)
    vocab_start = tensor_rank * vocab_block

    def embed_block(block_index):
        ids_here = vocab_start + block_index * step_rows + lax.iota(jnp.int32, step_rows)
        onehot = (ids_here[:, None] == ids_all[None, :]).astype(jnp.bfloat16)
        summed = jnp.dot(onehot, embed_all, preferred_element_type=jnp.float32)
        tallies = jnp.sum(onehot, axis=1, dtype=jnp.float32)
        return (summed, tallies)

    block_sums, block_counts = lax.map(
        embed_block, jnp.arange(vocab_block // step_rows, dtype=jnp.int32)
    )
    embed_sum = block_sums.reshape(vocab_block, col_block)
    counts = block_counts.reshape(vocab_block)
    divisor = factor_decay * old_embed_diag + (1.0 - factor_decay) * (counts / tokens_all) + damping
    precond_embed = learning_rate * embed_sum / divisor[:, None]
    return (precond_attn, precond_router, precond_norms, precond_embed)


def solution(mesh):
    return jax.shard_map(
        per_device,
        mesh=mesh,
        in_specs=(
            P(None, "shard", ("tensor", "section")),
            P(None, "shard"),
            P("shard"),
            P(None, "shard", ("tensor", "section")),
            P("shard", "tensor", "section"),
            P(),
            P(None, ("tensor", "section")),
            P("tensor"),
        ),
        out_specs=(
            P(None, "tensor", "section"),
            P(None, "tensor"),
            P(None, ("tensor", "section")),
            P("tensor", "section"),
        ),
        check_vma=False,
    )
```

profile of v0, /device:TPU:8, one launch (start us, length us, event | category | flops | bytes accessed | tf_op | source)
XLA Modules:
  0.0 1097.6 jit_solution(1544421095464947552)
XLA Ops:
  8.0 450.4 %while.26 = (s32[]{:T(128)}, bf16[8,256,576]{1,2,0:T(8,128)(2,1)S(1)}, bf16[8,256,288]{1,2,0:T(8,128)(2,1)S(1)}, bf16[8,256,72]{1,2,0:T(8,128)(2,1)}, s32[]{:T(128)}, /*index=5*/s32[]{:T(128)}, s32[]{:T(128)}) while((s32[]{:T(128)}, bf16[8,256,576]{1,2,0:T(8,128)(2,1)S(1)}, bf16[8,256,288]{1,2,0:T(8,128)(2,1)S(1)}, ...), condition=%wide.region_1.2_spmd, body=%wide.region_0.1_spmd.sunk | while | flops 2 | bytes 4608145 | solution.py:61
  8.1 1.4 constant_dynamic-slice_fusion.2
  9.5 56.6 %all-gather.27.cloned.1.call-done = bf16[1,256,2304]{1,2,0:T(8,128)(2,1)} async-done(((bf16[1,256,72]{1,2,0:T(8,128)(2,1)}), bf16[1,256,2304]{1,2,0:T(8,128)(2,1)}) %all-gather.27.cloned.1.call-update) | async-done | bytes 1179664 | tf_op jit(solution)/shard_map/while/body/eval_jaxpr/all_gather | solution.py:56
  69.5 52.5 %all-gather.27.cloned.1.call-done = bf16[1,256,2304]{1,2,0:T(8,128)(2,1)} async-done(((bf16[1,256,72]{1,2,0:T(8,128)(2,1)}), bf16[1,256,2304]{1,2,0:T(8,128)(2,1)}) %all-gather.27.cloned.1.call-update) | async-done | bytes 1179664 | tf_op jit(solution)/shard_map/while/body/eval_jaxpr/all_gather | solution.py:56
  125.4 52.5 %all-gather.27.cloned.1.call-done = bf16[1,256,2304]{1,2,0:T(8,128)(2,1)} async-done(((bf16[1,256,72]{1,2,0:T(8,128)(2,1)}), bf16[1,256,2304]{1,2,0:T(8,128)(2,1)}) %all-gather.27.cloned.1.call-update) | async-done | bytes 1179664 | tf_op jit(solution)/shard_map/while/body/eval_jaxpr/all_gather | solution.py:56
  181.3 52.2 %all-gather.27.cloned.1.call-done = bf16[1,256,2304]{1,2,0:T(8,128)(2,1)} async-done(((bf16[1,256,72]{1,2,0:T(8,128)(2,1)}), bf16[1,256,2304]{1,2,0:T(8,128)(2,1)}) %all-gather.27.cloned.1.call-update) | async-done | bytes 1179664 | tf_op jit(solution)/shard_map/while/body/eval_jaxpr/all_gather | solution.py:56
  236.9 52.2 %all-gather.27.cloned.1.call-done = bf16[1,256,2304]{1,2,0:T(8,128)(2,1)} async-done(((bf16[1,256,72]{1,2,0:T(8,128)(2,1)}), bf16[1,256,2304]{1,2,0:T(8,128)(2,1)}) %all-gather.27.cloned.1.call-update) | async-done | bytes 1179664 | tf_op jit(solution)/shard_map/while/body/eval_jaxpr/all_gather | solution.py:56
  292.5 52.2 %all-gather.27.cloned.1.call-done = bf16[1,256,2304]{1,2,0:T(8,128)(2,1)} async-done(((bf16[1,256,72]{1,2,0:T(8,128)(2,1)}), bf16[1,256,2304]{1,2,0:T(8,128)(2,1)}) %all-gather.27.cloned.1.call-update) | async-done | bytes 1179664 | tf_op jit(solution)/shard_map/while/body/eval_jaxpr/all_gather | solution.py:56
  348.1 52.5 %all-gather.27.cloned.1.call-done = bf16[1,256,2304]{1,2,0:T(8,128)(2,1)} async-done(((bf16[1,256,72]{1,2,0:T(8,128)(2,1)}), bf16[1,256,2304]{1,2,0:T(8,128)(2,1)}) %all-gather.27.cloned.1.call-update) | async-done | bytes 1179664 | tf_op jit(solution)/shard_map/while/body/eval_jaxpr/all_gather | solution.py:56
  404.0 52.5 %all-gather.27.cloned.1.call-done = bf16[1,256,2304]{1,2,0:T(8,128)(2,1)} async-done(((bf16[1,256,72]{1,2,0:T(8,128)(2,1)}), bf16[1,256,2304]{1,2,0:T(8,128)(2,1)}) %all-gather.27.cloned.1.call-update) | async-done | bytes 1179664 | tf_op jit(solution)/shard_map/while/body/eval_jaxpr/all_gather | solution.py:56
  458.5 3.7 fusion.83
  462.3 70.5 %reduce-scatter.2.cloned.1.call-done = f32[1,576,288]{1,2,0:T(8,128)} async-done(((f32[8,576,288]{1,2,0:T(8,128)}), f32[1,576,288]{1,2,0:T(8,128)}) %reduce-scatter.2.cloned.1.call-update) | async-done | bytes 663568 | tf_op jit(solution)/shard_map/reduce_scatter | solution.py:65
  532.8 2.1 fusion.48
  534.9 69.3 %psum.56 = f32[1]{0:T(128)} all-reduce(f32[1]{0:T(128)} %bitcast.4), channel_id=1, replica_groups=mesh['shard'=8,'tensor'=4,'section'=8] {'tensor','section'}, use_global_device_ids=true, to_apply=%region_4.5 | all-reduce | flops 1 | bytes 8 | tf_op jit(solution)/shard_map/psum | solution.py:71
  605.1 1.9 copy.32
  607.7 65.6 %all-gather.19.cloned.1.call-done = bf16[1,2304,288]{2,0,1:T(2,128)(2,1)} async-done(((bf16[1,576,288]{2,0,1:T(2,128)(2,1)}), bf16[1,2304,288]{2,0,1:T(2,128)(2,1)}) %all-gather.19.cloned.1.call-update) | async-done | bytes 1327120 | tf_op jit(solution)/shard_map/all_gather | solution.py:78
  673.3 8.4 copy.33
  681.7 29.2 %all-gather.17.cloned.1.call-done = bf16[1,576,2304]{1,2,0:T(8,128)(2,1)} async-done(((bf16[1,576,288]{1,2,0:T(8,128)(2,1)}), bf16[1,576,2304]{1,2,0:T(8,128)(2,1)}) %all-gather.17.cloned.1.call-update) | async-done | bytes 2654224 | tf_op jit(solution)/shard_map/all_gather | solution.py:79
  710.9 3.8 fusion.29
  715.5 41.7 %all-gather.25.cloned.1.call-done = bf16[4,576,288]{1,2,0:T(8,128)(2,1)} async-done(((bf16[1,576,288]{1,2,0:T(8,128)(2,1)}), bf16[4,576,288]{1,2,0:T(8,128)(2,1)}) %all-gather.25.cloned.1.call-update) | async-done | bytes 1327120 | tf_op jit(solution)/shard_map/all_gather | solution.py:80
  757.3 2.1 copy.34
  759.4 2.0 reshape.184
  761.4 24.7 %all-gather.15.cloned.1.call-done = bf16[1,576,2304]{1,2,0:T(8,128)(2,1)} async-done(((bf16[1,576,288]{1,2,0:T(8,128)(2,1)}), bf16[1,576,2304]{1,2,0:T(8,128)(2,1)}) %all-gather.15.cloned.1.call-update) | async-done | bytes 2654224 | tf_op jit(solution)/shard_map/all_gather | solution.py:81
  786.2 4.2 fusion.21
  790.6 19.7 %psum.60 = f32[8,8]{1,0:T(8,128)S(1)} all-reduce(f32[8,8]{1,0:T(8,128)S(1)} %fusion.84), channel_id=1, replica_groups=mesh['shard'=8,'tensor'=4,'section'=8] {'shard'}, use_global_device_ids=true, to_apply=%region_8.9 | all-reduce | flops 64 | bytes 512 | tf_op jit(solution)/shard_map/psum | solution.py:102
  812.3 15.1 %all-gather.4 = s32[8,1,256]{2,1,0:T(1,128)S(1)} all-gather(s32[1,1,256]{2,1,0:T(1,128)S(1)} %bitcast.152), channel_id=1, replica_groups=mesh['shard'=8,'tensor'=4,'section'=8] {'shard'}, dimensions={0}, use_global_device_ids=true | all-gather | bytes 9216 | tf_op jit(solution)/shard_map/all_gather | solution.py:124
  827.8 9.9 all-gather.21.cloned.1.call-done
  837.7 2.0 fusion.44
  839.7 2.0 fusion.43
  841.7 2.0 fusion.42
  843.7 2.0 fusion.41
  845.6 2.0 fusion.40
  847.6 56.9 %all-reduce.6 = bf16[5,256,288]{1,2,0:T(8,128)(2,1)S(1)} all-reduce(f32[5,256,288]{1,2,0:T(8,128)} %fusion.40), channel_id=1, replica_groups=mesh['shard'=8,'tensor'=4,'section'=8] {'tensor'}, use_global_device_ids=true, to_apply=%region_6.7 | all-reduce | flops 368640 | bytes 2211840 | tf_op jit(solution)/shard_map/psum | solution.py:97
  905.2 1.4 convolution_bitcast_fusion.2
  906.7 1.4 convolution_bitcast_fusion.1
  908.1 1.4 convolution_bitcast_fusion
  909.7 48.6 %all-reduce.7 = bf16[3,256,576]{1,2,0:T(8,128)(2,1)S(1)} all-reduce(f32[3,256,576]{1,2,0:T(8,128)S(1)} %pad_maximum_fusion), channel_id=1, replica_groups=mesh['shard'=8,'tensor'=4,'section'=8] {'section'}, use_global_device_ids=true, to_apply=%region_5.6 | all-reduce | flops 442368 | bytes 2654208 | tf_op jit(solution)/shard_map/psum | solution.py:90
  958.6 33.9 %all-reduce = (f32[8,576]{1,0:T(8,128)S(1)}, f32[2,72]{1,0:T(2,128)S(1)}, f32[2,72]{1,0:T(2,128)S(1)}) all-reduce(f32[8,576]{1,0:T(8,128)S(1)} %fusion.45, f32[2,72]{1,0:T(2,128)S(1)} %get-tuple-element.173, f32[2,72]{1,0:T(2,128)S(1)} %get-tuple-element.172), channel_id=1, replica_groups=mesh['shard'=8,'tensor'=4,'section'=8] {'shard'}, use_global_device_ids=true, to_apply=%region_10.11 | all-reduce | flops 4896 | bytes 39168 | tf_op jit(solution)/shard_map/psum | solution.py:131
  993.1 2.3 fusion.34
  996.6 2.5 copy.35
  999.2 17.1 %while.27 = (s32[]{:T(128)}, f32[4,512,288]{1,2,0:T(8,128)S(1)}, f32[4,512]{1,0:T(4,128)S(1)}, s32[4]{0:T(128)S(1)}, s32[]{:T(128)}, /*index=5*/s32[2048]{0:T(10...) while((s32[]{:T(128)}, f32[4,512,288]{1,2,0:T(8,128)S(1)}, f32[4,512]{1,0:T(4,128)S(1)}, ...), condition=%wide.region_17.18_spmd, body=%wide.region_15.17_spmd.sunk | while | flops 609222656 | bytes 1798293 | solution.py:145
  1000.3 2.5 fusion.99
  1004.5 2.5 fusion.99
  1008.8 2.5 fusion.99
  1013.1 2.5 fusion.99
  1017.2 1.7 broadcast_divide_fusion
  1018.9 67.6 %all-reduce.5.cloned.1.call-done = f32[4,576,288]{1,2,0:T(8,128)} async-done(((f32[4,576,288]{1,2,0:T(8,128)}), f32[4,576,288]{1,2,0:T(8,128)}) %all-reduce.5.cloned.1.call-update) | async-done | bytes 2654224 | tf_op jit(solution)/shard_map/psum | solution.py:131
  1086.5 3.7 broadcast_multiply_fusion
  (127 shorter events, 37.7 us)
Async XLA Ops:
  8.0 782.5 %copy-start = (bf16[8,256]{1,0:T(8,128)(2,1)S(1)}, bf16[8,256]{1,0:T(8,128)(2,1)}, u32[]{:S(2)}) copy-start(bf16[8,256]{1,0:T(8,128)(2,1)} %param.13) | copy-start | bytes 12292
  8.1 58.1 %all-gather.27.cloned.1.call-start = ((), (), s32[]{:S(2)}) async-start(), calls=%async_computation.9 | async-start | bytes 1216512 | tf_op jit(solution)/shard_map/while/body/eval_jaxpr/all_gather | solution.py:56
  68.0 54.0 %all-gather.27.cloned.1.call-start = ((), (), s32[]{:S(2)}) async-start(), calls=%async_computation.9 | async-start | bytes 1216512 | tf_op jit(solution)/shard_map/while/body/eval_jaxpr/all_gather | solution.py:56
  124.0 54.0 %all-gather.27.cloned.1.call-start = ((), (), s32[]{:S(2)}) async-start(), calls=%async_computation.9 | async-start | bytes 1216512 | tf_op jit(solution)/shard_map/while/body/eval_jaxpr/all_gather | solution.py:56
  179.9 53.7 %all-gather.27.cloned.1.call-start = ((), (), s32[]{:S(2)}) async-start(), calls=%async_computation.9 | async-start | bytes 1216512 | tf_op jit(solution)/shard_map/while/body/eval_jaxpr/all_gather | solution.py:56
  235.4 53.7 %all-gather.27.cloned.1.call-start = ((), (), s32[]{:S(2)}) async-start(), calls=%async_computation.9 | async-start | bytes 1216512 | tf_op jit(solution)/shard_map/while/body/eval_jaxpr/all_gather | solution.py:56
  291.0 53.7 %all-gather.27.cloned.1.call-start = ((), (), s32[]{:S(2)}) async-start(), calls=%async_computation.9 | async-start | bytes 1216512 | tf_op jit(solution)/shard_map/while/body/eval_jaxpr/all_gather | solution.py:56
  346.6 54.0 %all-gather.27.cloned.1.call-start = ((), (), s32[]{:S(2)}) async-start(), calls=%async_computation.9 | async-start | bytes 1216512 | tf_op jit(solution)/shard_map/while/body/eval_jaxpr/all_gather | solution.py:56
  402.5 54.0 %all-gather.27.cloned.1.call-start = ((), (), s32[]{:S(2)}) async-start(), calls=%async_computation.9 | async-start | bytes 1216512 | tf_op jit(solution)/shard_map/while/body/eval_jaxpr/all_gather | solution.py:56
  458.4 3.7 copy-start.5
  458.5 3.7 copy-start.7
  458.5 74.3 %reduce-scatter.2.cloned.1.call-start = ((), (), s32[]{:S(2)}) async-start(), calls=%async_computation.1 | async-start | bytes 6635520 | tf_op jit(solution)/shard_map/reduce_scatter | solution.py:65
  462.2 70.6 %copy-start.8 = (f32[1,576,288]{1,2,0:T(8,128)S(1)}, f32[1,576,288]{1,2,0:T(8,128)}, u32[]{:S(2)}) copy-start(f32[1,576,288]{1,2,0:T(8,128)} %param.16) | copy-start | bytes 1990660
  462.2 211.0 %all-gather.19.cloned.1.call-start = ((), (), s32[]{:S(2)}) async-start(), calls=%async_computation.4 | async-start | bytes 4423680 | tf_op jit(solution)/shard_map/all_gather | solution.py:78
  534.9 72.2 %copy-start.1 = (bf16[1,576,288]{1,2,0:T(8,128)(2,1)}, bf16[1,576,288]{1,2,0:T(8,128)(2,1)S(1)}, u32[]{:S(2)}) copy-start(bf16[1,576,288]{1,2,0:T(8,128)(2,1)S(1)} %get-tuple-element.206) | copy-start | bytes 995332
  605.1 76.6 %copy-start.3 = (bf16[1,576,288]{1,2,0:T(8,128)(2,1)}, bf16[1,576,288]{1,2,0:T(8,128)(2,1)S(1)}, u32[]{:S(2)}) copy-start(bf16[1,576,288]{1,2,0:T(8,128)(2,1)S(1)} %fusion.50) | copy-start | bytes 995332
  607.1 103.9 %all-gather.17.cloned.1.call-start = ((), (), s32[]{:S(2)}) async-start(), calls=%async_computation.3 | async-start | bytes 3317760 | tf_op jit(solution)/shard_map/all_gather | solution.py:79
  607.6 149.7 %all-gather.25.cloned.1.call-start = ((), (), s32[]{:S(2)}) async-start(), calls=%async_computation.8 | async-start | bytes 1843200 | tf_op jit(solution)/shard_map/all_gather | solution.py:80
  714.7 71.4 %all-gather.15.cloned.1.call-start = ((), (), s32[]{:S(2)}) async-start(), calls=%async_computation.2 | async-start | bytes 3317760 | tf_op jit(solution)/shard_map/all_gather | solution.py:81
  715.5 70.7 %copy-start.2 = (bf16[1,576,288]{1,2,0:T(8,128)(2,1)S(1)}, bf16[1,576,288]{1,2,0:T(8,128)(2,1)}, u32[]{:S(2)}) copy-start(bf16[1,576,288]{1,2,0:T(8,128)(2,1)} %copy-done.1) | copy-start | bytes 995332
  715.5 122.2 %all-gather.21.cloned.1.call-start = ((), (), s32[]{:S(2)}) async-start(), calls=%async_computation.5 | async-start | bytes 3317760 | tf_op jit(solution)/shard_map/all_gather | solution.py:83
  761.4 48.9 %copy-start.11 = (f32[8,8]{1,0:T(8,128)S(1)}, f32[8,8]{1,0:T(8,128)}, u32[]{:S(2)}) copy-start(f32[8,8]{1,0:T(8,128)} %param.17) | copy-start | bytes 772
  761.4 50.8 %copy-start.12 = (s32[256]{0:T(256)S(1)}, s32[256]{0:T(256)}, u32[]{:S(2)}) copy-start(s32[256]{0:T(256)} %param.14) | copy-start | bytes 3076
  761.4 65.9 %copy-start.9 = (bf16[2,256,72]{1,2,0:T(8,128)(2,1)S(1)}, bf16[2,256,72]{1,2,0:T(8,128)(2,1)}, u32[]{:S(2)}) copy-start(bf16[2,256,72]{1,2,0:T(8,128)(2,1)} %param.15) | copy-start | bytes 221188
  761.4 76.3 %copy-start.6 = (bf16[8,256,576]{1,2,0:T(8,128)(2,1)S(1)}, bf16[8,256,576]{1,2,0:T(8,128)(2,1)}, u32[]{:S(2)}) copy-start(bf16[8,256,576]{1,2,0:T(8,128)(2,1)} %copy-done.5) | copy-start | bytes 7077892
  790.4 206.2 %all-gather.23.cloned.1.call-start = ((), (), s32[]{:S(2)}) async-start(), calls=%async_computation.7 | async-start | bytes 1327104 | tf_op jit(solution)/shard_map/all_gather | solution.py:125
  905.2 181.3 %all-reduce.5.cloned.1.call-start = ((), (), s32[]{:S(2)}) async-start(), calls=%async_computation.6 | async-start | bytes 5898240 | tf_op jit(solution)/shard_map/psum | solution.py:131
  995.4 0.7 copy-start.13
  995.4 3.8 copy-start.4
  1016.5 0.7 copy-start.10
Sparse Core Ops, SparseCore 0:
  12.1 53.9 all-gather.26
  72.1 49.8 all-gather.26
  128.0 49.8 all-gather.26
  183.6 49.8 all-gather.26
  239.2 49.8 all-gather.26
  294.8 49.8 all-gather.26
  350.7 49.8 all-gather.26
  406.6 49.8 all-gather.26
Sparse Core Ops, SparseCore 1:
  462.3 70.4 reduce-scatter.1
  607.1 66.1 all-gather.18
  675.1 35.8 all-gather.16
  714.8 42.4 all-gather.24
  759.3 26.8 all-gather.14
  790.5 47.2 all-gather.20
  905.3 39.6 all-gather.22
  995.5 90.9 all-reduce.4
where the time goes:
time: 1100 us
  waiting for transfers between devices  734 us (67%)
  blocking collectives  243 us (22%)
  local copies, waits for them, and re-layouts  48.5 us (4%)
  matrix products  38.8 us (4%)
  between operations  17.2 us (2%)
  other arithmetic  12.2 us (1%)
    all_gather x8, waiting for transfers between devices, collect(): whole = lax.all_gather(piece, ('tensor', 'section'), axis=1, tiled=True)  423 us
    reduce_scatter x1, waiting for transfers between devices, per_device(): lax.psum_scatter(partial_value, 'shard', scatter_dimension=0, tiled=True)  70.5 us
    psum x1, blocking collectives, per_device(): trace = lax.psum(diag_part, ('tensor', 'section'))  69.3 us
    psum x1, waiting for transfers between devices, per_device(): attn_sum, router_total = lax.psum((attn_terms, router_term), 'shard')  67.6 us
    all_gather x1, waiting for transfers between devices, per_device(): first_cols = lax.all_gather(first_low, 'tensor', axis=1, tiled=True)  65.6 us
    psum x1, blocking collectives, per_device(): right = lax.psum(right_terms, 'tensor').astype(jnp.bfloat16)  56.9 us
    psum x1, blocking collectives, per_device(): left = lax.psum(left_terms, 'section').astype(jnp.bfloat16)  48.6 us
    all_gather x1, waiting for transfers between devices, per_device(): lax.all_gather(image.astype(jnp.bfloat16), 'tensor', axis=1, tiled=True)  41.7 us
  transfers between devices with their start and end apart: 16, of which 15 were waited for; matrix products, arithmetic and copies ran while one was open for 4% of the time, Pallas kernels for 0%

commit v1 on v0

--- a/solution.py
+++ b/solution.py
@@ -68,7 +68,7 @@
     eye_block = (row_index == col_index).astype(jnp.float32)
     matrix = factor_decay * old_factors + (1.0 - factor_decay) * fresh + damping * eye_block
     diag_part = jnp.sum(matrix * eye_block, axis=(1, 2))
-    trace = lax.psum(diag_part, ("tensor", "section"))
+    trace = lax.psum(lax.psum(diag_part, "tensor"), "section")
     factor_scale = (D / (3.0 * trace))[:, None, None]
     matrix_low = lax.optimization_barrier(matrix.astype(jnp.bfloat16))
     first = 2.0 * factor_scale * eye_block - factor_scale * factor_scale * matrix_low.astype(

time: 1100 us -> 1050 us (0.955)
  blocking collectives: 243 us -> 197 us
    psum x1 -> x2, blocking collectives: 69.3 us -> 23.1 us  [per_device(): trace = lax.psum(lax.psum(diag_part, 'tensor'), 'section')]
where the time goes in v1:
time: 1050 us
  waiting for transfers between devices  730 us (70%)
  blocking collectives  197 us (19%)
  local copies, waits for them, and re-layouts  49 us (5%)
  matrix products  38.8 us (4%)
  between operations  17.2 us (2%)
  other arithmetic  12.2 us (1%)
    all_gather x8, waiting for transfers between devices, collect(): whole = lax.all_gather(piece, ('tensor', 'section'), axis=1, tiled=True)  423 us
    reduce_scatter x1, waiting for transfers between devices, per_device(): lax.psum_scatter(partial_value, 'shard', scatter_dimension=0, tiled=True)  70.5 us
    psum x1, waiting for transfers between devices, per_device(): attn_sum, router_total = lax.psum((attn_terms, router_term), 'shard')  66.7 us
    all_gather x1, waiting for transfers between devices, per_device(): first_cols = lax.all_gather(first_low, 'tensor', axis=1, tiled=True)  62.6 us
    psum x1, blocking collectives, per_device(): right = lax.psum(right_terms, 'tensor').astype(jnp.bfloat16)  58.1 us
    psum x1, blocking collectives, per_device(): left = lax.psum(left_terms, 'section').astype(jnp.bfloat16)  48.5 us
    all_gather x1, waiting for transfers between devices, per_device(): lax.all_gather(image.astype(jnp.bfloat16), 'tensor', axis=1, tiled=True)  41.7 us
    psum x1, blocking collectives, per_device(): attn_sum, router_total = lax.psum((attn_terms, router_term), 'shard')  32.5 us
  transfers between devices with their start and end apart: 16, of which 15 were waited for; matrix products, arithmetic and copies ran while one was open for 4% of the time, Pallas kernels for 0%

profile of v1, /device:TPU:8, one launch (start us, length us, event | category | flops | bytes accessed | tf_op | source)
XLA Modules:
  0.0 1048.2 jit_solution(550658560823328849)
XLA Ops:
  8.0 450.4 %while.26 = (s32[]{:T(128)}, bf16[8,256,576]{1,2,0:T(8,128)(2,1)S(1)}, bf16[8,256,288]{1,2,0:T(8,128)(2,1)S(1)}, bf16[8,256,72]{1,2,0:T(8,128)(2,1)}, s32[]{:T(128)}, /*index=5*/s32[]{:T(128)}, s32[]{:T(128)}) while((s32[]{:T(128)}, bf16[8,256,576]{1,2,0:T(8,128)(2,1)S(1)}, bf16[8,256,288]{1,2,0:T(8,128)(2,1)S(1)}, ...), condition=%wide.region_1.2_spmd, body=%wide.region_0.1_spmd.sunk | while | flops 2 | bytes 4608145 | solution.py:61
  9.5 56.6 %all-gather.27.cloned.1.call-done = bf16[1,256,2304]{1,2,0:T(8,128)(2,1)} async-done(((bf16[1,256,72]{1,2,0:T(8,128)(2,1)}), bf16[1,256,2304]{1,2,0:T(8,128)(2,1)}) %all-gather.27.cloned.1.call-update) | async-done | bytes 1179664 | tf_op jit(solution)/shard_map/while/body/eval_jaxpr/all_gather | solution.py:56
  69.5 52.5 %all-gather.27.cloned.1.call-done = bf16[1,256,2304]{1,2,0:T(8,128)(2,1)} async-done(((bf16[1,256,72]{1,2,0:T(8,128)(2,1)}), bf16[1,256,2304]{1,2,0:T(8,128)(2,1)}) %all-gather.27.cloned.1.call-update) | async-done | bytes 1179664 | tf_op jit(solution)/shard_map/while/body/eval_jaxpr/all_gather | solution.py:56
  125.4 52.5 %all-gather.27.cloned.1.call-done = bf16[1,256,2304]{1,2,0:T(8,128)(2,1)} async-done(((bf16[1,256,72]{1,2,0:T(8,128)(2,1)}), bf16[1,256,2304]{1,2,0:T(8,128)(2,1)}) %all-gather.27.cloned.1.call-update) | async-done | bytes 1179664 | tf_op jit(solution)/shard_map/while/body/eval_jaxpr/all_gather | solution.py:56
  181.3 52.2 %all-gather.27.cloned.1.call-done = bf16[1,256,2304]{1,2,0:T(8,128)(2,1)} async-done(((bf16[1,256,72]{1,2,0:T(8,128)(2,1)}), bf16[1,256,2304]{1,2,0:T(8,128)(2,1)}) %all-gather.27.cloned.1.call-update) | async-done | bytes 1179664 | tf_op jit(solution)/shard_map/while/body/eval_jaxpr/all_gather | solution.py:56
  236.9 52.2 %all-gather.27.cloned.1.call-done = bf16[1,256,2304]{1,2,0:T(8,128)(2,1)} async-done(((bf16[1,256,72]{1,2,0:T(8,128)(2,1)}), bf16[1,256,2304]{1,2,0:T(8,128)(2,1)}) %all-gather.27.cloned.1.call-update) | async-done | bytes 1179664 | tf_op jit(solution)/shard_map/while/body/eval_jaxpr/all_gather | solution.py:56
  292.5 52.2 %all-gather.27.cloned.1.call-done = bf16[1,256,2304]{1,2,0:T(8,128)(2,1)} async-done(((bf16[1,256,72]{1,2,0:T(8,128)(2,1)}), bf16[1,256,2304]{1,2,0:T(8,128)(2,1)}) %all-gather.27.cloned.1.call-update) | async-done | bytes 1179664 | tf_op jit(solution)/shard_map/while/body/eval_jaxpr/all_gather | solution.py:56
  348.1 52.5 %all-gather.27.cloned.1.call-done = bf16[1,256,2304]{1,2,0:T(8,128)(2,1)} async-done(((bf16[1,256,72]{1,2,0:T(8,128)(2,1)}), bf16[1,256,2304]{1,2,0:T(8,128)(2,1)}) %all-gather.27.cloned.1.call-update) | async-done | bytes 1179664 | tf_op jit(solution)/shard_map/while/body/eval_jaxpr/all_gather | solution.py:56
  404.0 52.5 %all-gather.27.cloned.1.call-done = bf16[1,256,2304]{1,2,0:T(8,128)(2,1)} async-done(((bf16[1,256,72]{1,2,0:T(8,128)(2,1)}), bf16[1,256,2304]{1,2,0:T(8,128)(2,1)}) %all-gather.27.cloned.1.call-update) | async-done | bytes 1179664 | tf_op jit(solution)/shard_map/while/body/eval_jaxpr/all_gather | solution.py:56
  458.5 3.6 fusion.83
  462.3 70.5 %reduce-scatter.2.cloned.1.call-done = f32[1,576,288]{1,2,0:T(8,128)} async-done(((f32[8,576,288]{1,2,0:T(8,128)}), f32[1,576,288]{1,2,0:T(8,128)}) %reduce-scatter.2.cloned.1.call-update) | async-done | bytes 663568 | tf_op jit(solution)/shard_map/reduce_scatter | solution.py:65
  532.8 2.1 fusion.48
  534.9 12.4 %psum.63 = f32[1]{0:T(128)} all-reduce(f32[1]{0:T(128)} %bitcast.4), channel_id=1, replica_groups=mesh['shard'=8,'tensor'=4,'section'=8] {'tensor'}, use_global_device_ids=true, to_apply=%region_4.5 | all-reduce | flops 1 | bytes 8 | tf_op jit(solution)/shard_map/psum | solution.py:71
  547.3 10.6 %psum.64 = f32[1]{0:T(128)} all-reduce(f32[1]{0:T(128)} %psum.63), channel_id=1, replica_groups=mesh['shard'=8,'tensor'=4,'section'=8] {'section'}, use_global_device_ids=true, to_apply=%region_5.6 | all-reduce | flops 1 | bytes 8 | tf_op jit(solution)/shard_map/psum | solution.py:71
  558.8 1.9 copy.32
  561.4 62.6 %all-gather.19.cloned.1.call-done = bf16[1,2304,288]{2,0,1:T(2,128)(2,1)} async-done(((bf16[1,576,288]{2,0,1:T(2,128)(2,1)}), bf16[1,2304,288]{2,0,1:T(2,128)(2,1)}) %all-gather.19.cloned.1.call-update) | async-done | bytes 1327120 | tf_op jit(solution)/shard_map/all_gather | solution.py:78
  624.0 8.4 copy.33
  632.4 29.2 %all-gather.17.cloned.1.call-done = bf16[1,576,2304]{1,2,0:T(8,128)(2,1)} async-done(((bf16[1,576,288]{1,2,0:T(8,128)(2,1)}), bf16[1,576,2304]{1,2,0:T(8,128)(2,1)}) %all-gather.17.cloned.1.call-update) | async-done | bytes 2654224 | tf_op jit(solution)/shard_map/all_gather | solution.py:79
  661.7 3.8 fusion.29
  666.3 41.7 %all-gather.25.cloned.1.call-done = bf16[4,576,288]{1,2,0:T(8,128)(2,1)} async-done(((bf16[1,576,288]{1,2,0:T(8,128)(2,1)}), bf16[4,576,288]{1,2,0:T(8,128)(2,1)}) %all-gather.25.cloned.1.call-update) | async-done | bytes 1327120 | tf_op jit(solution)/shard_map/all_gather | solution.py:80
  708.0 2.1 copy.34
  710.2 2.0 reshape.184
  712.2 24.7 %all-gather.15.cloned.1.call-done = bf16[1,576,2304]{1,2,0:T(8,128)(2,1)} async-done(((bf16[1,576,288]{1,2,0:T(8,128)(2,1)}), bf16[1,576,2304]{1,2,0:T(8,128)(2,1)}) %all-gather.15.cloned.1.call-update) | async-done | bytes 2654224 | tf_op jit(solution)/shard_map/all_gather | solution.py:81
  736.9 4.2 fusion.21
  741.4 19.7 %psum.68 = f32[8,8]{1,0:T(8,128)S(1)} all-reduce(f32[8,8]{1,0:T(8,128)S(1)} %fusion.84), channel_id=1, replica_groups=mesh['shard'=8,'tensor'=4,'section'=8] {'shard'}, use_global_device_ids=true, to_apply=%region_9.10 | all-reduce | flops 64 | bytes 512 | tf_op jit(solution)/shard_map/psum | solution.py:102
  763.0 15.1 %all-gather.4 = s32[8,1,256]{2,1,0:T(1,128)S(1)} all-gather(s32[1,1,256]{2,1,0:T(1,128)S(1)} %bitcast.152), channel_id=1, replica_groups=mesh['shard'=8,'tensor'=4,'section'=8] {'shard'}, dimensions={0}, use_global_device_ids=true | all-gather | bytes 9216 | tf_op jit(solution)/shard_map/all_gather | solution.py:124
  778.5 10.0 all-gather.21.cloned.1.call-done
  788.5 2.0 fusion.44
  790.5 2.0 fusion.43
  792.5 2.0 fusion.42
  794.5 2.0 fusion.41
  796.4 2.0 fusion.40
  798.4 58.1 %all-reduce.6 = bf16[5,256,288]{1,2,0:T(8,128)(2,1)S(1)} all-reduce(f32[5,256,288]{1,2,0:T(8,128)} %fusion.40), channel_id=1, replica_groups=mesh['shard'=8,'tensor'=4,'section'=8] {'tensor'}, use_global_device_ids=true, to_apply=%region_7.8 | all-reduce | flops 368640 | bytes 2211840 | tf_op jit(solution)/shard_map/psum | solution.py:97
  857.3 1.4 convolution_bitcast_fusion.2
  858.7 1.4 convolution_bitcast_fusion.1
  860.1 1.4 convolution_bitcast_fusion
  861.7 48.5 %all-reduce.7 = bf16[3,256,576]{1,2,0:T(8,128)(2,1)S(1)} all-reduce(f32[3,256,576]{1,2,0:T(8,128)S(1)} %pad_maximum_fusion), channel_id=1, replica_groups=mesh['shard'=8,'tensor'=4,'section'=8] {'section'}, use_global_device_ids=true, to_apply=%region_6.7 | all-reduce | flops 442368 | bytes 2654208 | tf_op jit(solution)/shard_map/psum | solution.py:90
  910.6 32.5 %all-reduce = (f32[8,576]{1,0:T(8,128)S(1)}, f32[2,72]{1,0:T(2,128)S(1)}, f32[2,72]{1,0:T(2,128)S(1)}) all-reduce(f32[8,576]{1,0:T(8,128)S(1)} %fusion.45, f32[2,72]{1,0:T(2,128)S(1)} %get-tuple-element.173, f32[2,72]{1,0:T(2,128)S(1)} %get-tuple-element.172), channel_id=1, replica_groups=mesh['shard'=8,'tensor'=4,'section'=8] {'shard'}, use_global_device_ids=true, to_apply=%region_11.12 | all-reduce | flops 4896 | bytes 39168 | tf_op jit(solution)/shard_map/psum | solution.py:131
  943.7 2.3 fusion.34
  947.2 2.5 copy.35
  949.7 18.0 %while.27 = (s32[]{:T(128)}, f32[4,512,288]{1,2,0:T(8,128)S(1)}, f32[4,512]{1,0:T(4,128)S(1)}, s32[4]{0:T(128)S(1)}, s32[]{:T(128)}, /*index=5*/s32[2048]{0:T(10...) while((s32[]{:T(128)}, f32[4,512,288]{1,2,0:T(8,128)S(1)}, f32[4,512]{1,0:T(4,128)S(1)}, ...), condition=%wide.region_18.19_spmd, body=%wide.region_16.18_spmd.sunk | while | flops 609222656 | bytes 1798293 | solution.py:145
  951.1 2.5 fusion.99
  955.6 2.5 fusion.99
  960.1 2.5 fusion.99
  964.6 2.5 fusion.99
  968.7 1.7 broadcast_divide_fusion
  970.4 66.7 %all-reduce.5.cloned.1.call-done = f32[4,576,288]{1,2,0:T(8,128)} async-done(((f32[4,576,288]{1,2,0:T(8,128)}), f32[4,576,288]{1,2,0:T(8,128)}) %all-reduce.5.cloned.1.call-update) | async-done | bytes 2654224 | tf_op jit(solution)/shard_map/psum | solution.py:131
  1037.1 3.7 broadcast_multiply_fusion
  (128 shorter events, 39.5 us)
Async XLA Ops:
  8.0 733.2 %copy-start = (bf16[8,256]{1,0:T(8,128)(2,1)S(1)}, bf16[8,256]{1,0:T(8,128)(2,1)}, u32[]{:S(2)}) copy-start(bf16[8,256]{1,0:T(8,128)(2,1)} %param.13) | copy-start | bytes 12292
  8.1 58.1 %all-gather.27.cloned.1.call-start = ((), (), s32[]{:S(2)}) async-start(), calls=%async_computation.9 | async-start | bytes 1216512 | tf_op jit(solution)/shard_map/while/body/eval_jaxpr/all_gather | solution.py:56
  68.0 54.0 %all-gather.27.cloned.1.call-start = ((), (), s32[]{:S(2)}) async-start(), calls=%async_computation.9 | async-start | bytes 1216512 | tf_op jit(solution)/shard_map/while/body/eval_jaxpr/all_gather | solution.py:56
  124.0 54.0 %all-gather.27.cloned.1.call-start = ((), (), s32[]{:S(2)}) async-start(), calls=%async_computation.9 | async-start | bytes 1216512 | tf_op jit(solution)/shard_map/while/body/eval_jaxpr/all_gather | solution.py:56
  179.9 53.7 %all-gather.27.cloned.1.call-start = ((), (), s32[]{:S(2)}) async-start(), calls=%async_computation.9 | async-start | bytes 1216512 | tf_op jit(solution)/shard_map/while/body/eval_jaxpr/all_gather | solution.py:56
  235.4 53.7 %all-gather.27.cloned.1.call-start = ((), (), s32[]{:S(2)}) async-start(), calls=%async_computation.9 | async-start | bytes 1216512 | tf_op jit(solution)/shard_map/while/body/eval_jaxpr/all_gather | solution.py:56
  291.0 53.7 %all-gather.27.cloned.1.call-start = ((), (), s32[]{:S(2)}) async-start(), calls=%async_computation.9 | async-start | bytes 1216512 | tf_op jit(solution)/shard_map/while/body/eval_jaxpr/all_gather | solution.py:56
  346.6 54.0 %all-gather.27.cloned.1.call-start = ((), (), s32[]{:S(2)}) async-start(), calls=%async_computation.9 | async-start | bytes 1216512 | tf_op jit(solution)/shard_map/while/body/eval_jaxpr/all_gather | solution.py:56
  402.5 54.0 %all-gather.27.cloned.1.call-start = ((), (), s32[]{:S(2)}) async-start(), calls=%async_computation.9 | async-start | bytes 1216512 | tf_op jit(solution)/shard_map/while/body/eval_jaxpr/all_gather | solution.py:56
  458.4 3.7 copy-start.5
  458.5 3.7 copy-start.7
  458.5 74.3 %reduce-scatter.2.cloned.1.call-start = ((), (), s32[]{:S(2)}) async-start(), calls=%async_computation.1 | async-start | bytes 6635520 | tf_op jit(solution)/shard_map/reduce_scatter | solution.py:65
  462.2 70.6 %copy-start.8 = (f32[1,576,288]{1,2,0:T(8,128)S(1)}, f32[1,576,288]{1,2,0:T(8,128)}, u32[]{:S(2)}) copy-start(f32[1,576,288]{1,2,0:T(8,128)} %param.16) | copy-start | bytes 1990660
  462.2 161.8 %all-gather.19.cloned.1.call-start = ((), (), s32[]{:S(2)}) async-start(), calls=%async_computation.4 | async-start | bytes 4423680 | tf_op jit(solution)/shard_map/all_gather | solution.py:78
  534.9 26.0 %copy-start.1 = (bf16[1,576,288]{1,2,0:T(8,128)(2,1)}, bf16[1,576,288]{1,2,0:T(8,128)(2,1)S(1)}, u32[]{:S(2)}) copy-start(bf16[1,576,288]{1,2,0:T(8,128)(2,1)S(1)} %get-tuple-element.206) | copy-start | bytes 995332
  558.8 73.6 %copy-start.3 = (bf16[1,576,288]{1,2,0:T(8,128)(2,1)}, bf16[1,576,288]{1,2,0:T(8,128)(2,1)S(1)}, u32[]{:S(2)}) copy-start(bf16[1,576,288]{1,2,0:T(8,128)(2,1)S(1)} %fusion.50) | copy-start | bytes 995332
  560.8 100.9 %all-gather.17.cloned.1.call-start = ((), (), s32[]{:S(2)}) async-start(), calls=%async_computation.3 | async-start | bytes 3317760 | tf_op jit(solution)/shard_map/all_gather | solution.py:79
  561.4 146.7 %all-gather.25.cloned.1.call-start = ((), (), s32[]{:S(2)}) async-start(), calls=%async_computation.8 | async-start | bytes 1843200 | tf_op jit(solution)/shard_map/all_gather | solution.py:80
  665.5 71.4 %all-gather.15.cloned.1.call-start = ((), (), s32[]{:S(2)}) async-start(), calls=%async_computation.2 | async-start | bytes 3317760 | tf_op jit(solution)/shard_map/all_gather | solution.py:81
  666.2 70.7 %copy-start.2 = (bf16[1,576,288]{1,2,0:T(8,128)(2,1)S(1)}, bf16[1,576,288]{1,2,0:T(8,128)(2,1)}, u32[]{:S(2)}) copy-start(bf16[1,576,288]{1,2,0:T(8,128)(2,1)} %copy-done.1) | copy-start | bytes 995332
  666.2 122.3 %all-gather.21.cloned.1.call-start = ((), (), s32[]{:S(2)}) async-start(), calls=%async_computation.5 | async-start | bytes 3317760 | tf_op jit(solution)/shard_map/all_gather | solution.py:83
  712.2 48.9 %copy-start.11 = (f32[8,8]{1,0:T(8,128)S(1)}, f32[8,8]{1,0:T(8,128)}, u32[]{:S(2)}) copy-start(f32[8,8]{1,0:T(8,128)} %param.17) | copy-start | bytes 772
  712.2 50.8 %copy-start.12 = (s32[256]{0:T(256)S(1)}, s32[256]{0:T(256)}, u32[]{:S(2)}) copy-start(s32[256]{0:T(256)} %param.14) | copy-start | bytes 3076
  712.2 66.0 %copy-start.9 = (bf16[2,256,72]{1,2,0:T(8,128)(2,1)S(1)}, bf16[2,256,72]{1,2,0:T(8,128)(2,1)}, u32[]{:S(2)}) copy-start(bf16[2,256,72]{1,2,0:T(8,128)(2,1)} %param.15) | copy-start | bytes 221188
  712.2 76.3 %copy-start.6 = (bf16[8,256,576]{1,2,0:T(8,128)(2,1)S(1)}, bf16[8,256,576]{1,2,0:T(8,128)(2,1)}, u32[]{:S(2)}) copy-start(bf16[8,256,576]{1,2,0:T(8,128)(2,1)} %copy-done.5) | copy-start | bytes 7077892
  741.2 206.1 %all-gather.23.cloned.1.call-start = ((), (), s32[]{:S(2)}) async-start(), calls=%async_computation.7 | async-start | bytes 1327104 | tf_op jit(solution)/shard_map/all_gather | solution.py:125
  857.2 179.9 %all-reduce.5.cloned.1.call-start = ((), (), s32[]{:S(2)}) async-start(), calls=%async_computation.6 | async-start | bytes 5898240 | tf_op jit(solution)/shard_map/psum | solution.py:131
  946.0 0.7 copy-start.13
  946.0 3.8 copy-start.4
  968.0 0.7 copy-start.10
Sparse Core Ops, SparseCore 0:
  12.1 53.9 all-gather.26
  72.1 49.8 all-gather.26
  128.0 49.8 all-gather.26
  183.6 49.8 all-gather.26
  239.2 49.8 all-gather.26
  294.8 49.8 all-gather.26
  350.7 49.8 all-gather.26
  406.6 49.8 all-gather.26
Sparse Core Ops, SparseCore 1:
  462.3 70.4 reduce-scatter.1
  560.9 63.1 all-gather.18
  625.9 35.8 all-gather.16
  665.6 42.4 all-gather.24
  710.0 26.8 all-gather.14
  741.2 47.2 all-gather.20
  857.3 38.1 all-gather.22
  946.1 91.0 all-reduce.4
